TPU v7x, 32 devices: a whole 2x2x4 slice. The times are simulated.
32 devices in a mesh: grp: 2 (over y), chan: 4 (over z), sub: 4 (over x, core).
Axes of the slice: x: 2, y: 2, z: 4, core: 2. Of those that a mesh axis runs over, the one named last changes fastest.
Arguments:
- voltages: bfloat16 [2048, 2, 5504], P(('grp', 'chan', 'sub')), parts along dimension 0, may hold values from -6 to 6
- taps: float32 [1536], replicated, may hold values from -0.15625 to 0.15625
- input_id: int32 [1024], replicated, may hold values from 0 to 1023, each once
- counts: int32 [8], P('grp'), parts along dimension 0, may hold values from 2 to 8, as said below
- delays: int32 [512, 1024], P(('grp', 'sub')), parts along dimension 0, may hold values from 0 to 127
- beam_owner: int32 [512, 1], P('grp'), parts along dimension 0, may hold values from 0 to 3; in each aligned block of 64 rows (0 to 63, 64 to 127, ...) at most 32 rows name the same one
Outputs:
- visibility: bfloat16 [256, 2, 1024, 1024], P(('grp', 'chan'), None, 'sub'), parts along dimension 0
- resynth: float32 [1024, 2, 5504], P(('grp', 'chan', 'sub')), parts along dimension 0
There are 2 independent parts, one for each index of `grp`. A program takes and returns all parts, laid end to end along the dimension named above; an argument that names none is the same for every part. Nothing has to cross between parts.
Inputs may be any that keep to these rules, and one draw needn't show every extreme that they name: `input_id`: each input id appears once. `counts`: every draw has a block with all 8 spectra valid. `beam_owner`: within each section of 64 consecutive beams no owner is named more than 32 times; some owner is named exactly 32 times in some section.
All inputs are finite; a program needn't handle non-finite values.
Results may differ from a plain program's by a relative error of at most 0.007.
Values may be sent and summed in bfloat16 or wider, within the bound.
A program may use at most 192 MiB of HBM per device.

v0:
```python
import math
import jax
import jax.numpy as jnp
from jax import lax
from jax.sharding import PartitionSpec as P

NCH = 128
TAPS = 12
SPEC = 8
BLOCKS = 4
BEAMS = 256


def filter_table(taps, chans):
    length = taps.shape[0]
    position = jnp.arange(length, dtype=jnp.int32) % chans
    channel = jnp.arange(chans, dtype=jnp.int32)
    phase = (position[:, None] * channel[None, :] % chans).astype(jnp.float32) * (
        2.0 * math.pi / chans
    )
    cosine = taps[:, None] * jnp.cos(phase)
    sine = taps[:, None] * jnp.sin(phase)
    upper = jnp.concatenate([cosine, -sine], axis=1)
    lower = jnp.concatenate([sine, cosine], axis=1)
    return jnp.concatenate([upper, lower], axis=0).astype(jnp.bfloat16)


def resynthesize(received, table, taps_count, chans):
    count = received.shape[0]
    spectra_n = received.shape[3]
    table3 = table.reshape(2 * taps_count * chans, 2, chans)
    grid = jnp.einsum("pcht,mch->ptm", received, table3, preferred_element_type=jnp.float32)
    grid = grid.reshape(count, spectra_n, 2, taps_count, chans)
    total = jnp.zeros((count, spectra_n + taps_count - 1, 2, chans), jnp.float32)
    for k in range(taps_count):
        total = total + jnp.pad(
            grid[:, :, :, k, :], ((0, 0), (k, taps_count - 1 - k), (0, 0), (0, 0))
        )
    return jnp.transpose(total, (0, 2, 1, 3)).reshape(
        count, 2, (spectra_n + taps_count - 1) * chans
    )


def local(voltages, taps, input_id, counts, delays, beam_owner):
    n_chan = lax.axis_size("chan")
    n_sub = lax.axis_size("sub")
    inp_dev = voltages.shape[0]
    inputs = input_id.shape[0]
    chans = NCH
    taps_count = TAPS
    spectra_n = BLOCKS * SPEC
    ch_dev = chans // n_chan
    rows = inputs // n_sub
    section = BEAMS // n_sub
    most = min(section, max(2, 2 * section // n_chan))
    table = filter_table(taps, chans)
    position = jnp.arange(spectra_n, dtype=jnp.int32)
    valid = (position % SPEC < jnp.repeat(counts, SPEC)).astype(jnp.float32)
    total = jnp.sum(counts.astype(jnp.float32))
    frames = voltages.reshape(inp_dev, 2, spectra_n + taps_count - 1, chans)
    windows = jnp.concatenate(
        [frames[:, :, k : k + spectra_n, :] for k in range(taps_count)], axis=3
    )
    table3 = table.reshape(2, taps_count * chans, 2 * chans)
    filtered = jnp.einsum("icth,chm->mit", windows, table3, preferred_element_type=jnp.float32)
    filtered = filtered * valid[None, None, :]
    spectra = filtered.reshape(2, chans, inp_dev, spectra_n).astype(jnp.bfloat16)
    slot_of = jnp.zeros((inputs,), jnp.int32).at[input_id].set(jnp.arange(inputs, dtype=jnp.int32))
    turned = lax.all_to_all(spectra, "chan", split_axis=1, concat_axis=2, tiled=True)
    gathered = lax.all_gather(turned, "sub", axis=2, tiled=True)
    chan_part = slot_of // (n_sub * inp_dev)
    sub_part = slot_of // inp_dev % n_sub
    order = (sub_part * n_chan + chan_part) * inp_dev + slot_of % inp_dev
    by_id = jnp.take(gathered, order, axis=2)
    sub_index = lax.axis_index("sub")
    mine = lax.dynamic_slice_in_dim(by_id, sub_index * rows, rows, 2)
    real_part = jnp.einsum("cxit,cxjt->xij", mine, by_id, preferred_element_type=jnp.float32)
    imag_part = jnp.einsum("xit,xjt->xij", mine[1], by_id[0], preferred_element_type=jnp.float32)
    imag_part = imag_part - jnp.einsum(
        "xit,xjt->xij", mine[0], by_id[1], preferred_element_type=jnp.float32
    )
    visibility = (jnp.stack([real_part, imag_part], axis=1) / total).astype(jnp.bfloat16)
    channel = lax.axis_index("chan") * ch_dev + jnp.arange(ch_dev, dtype=jnp.int32)
    phase = (delays[None, :, :] * channel[:, None, None] % chans).astype(jnp.float32) * (
        2.0 * math.pi / chans
    )
    scale = 1.0 / math.sqrt(inputs)
    weight_cos = (jnp.cos(phase) * scale).astype(jnp.bfloat16)
    weight_sin = (jnp.sin(phase) * scale).astype(jnp.bfloat16)
    from_cos = jnp.einsum("xbi,cxit->cxbt", weight_cos, by_id, preferred_element_type=jnp.float32)
    from_sin = jnp.einsum("xbi,cxit->cxbt", weight_sin, by_id, preferred_element_type=jnp.float32)
    beams = jnp.stack([from_cos[0] - from_sin[1], from_cos[1] + from_sin[0]]).astype(jnp.bfloat16)
    owner = lax.dynamic_slice_in_dim(beam_owner[:, 0], sub_index * section, section)
    beam = jnp.arange(section, dtype=jnp.int32)
    earlier = (owner[None, :] == owner[:, None]) & (beam[None, :] < beam[:, None])
    rank = jnp.sum(earlier.astype(jnp.int32), axis=1)
    target = owner * most + rank
    select = (jnp.arange(n_chan * most, dtype=jnp.int32)[:, None] == target[None, :]).astype(
        jnp.bfloat16
    )
    placed = jnp.einsum("pb,cxbt->pcxt", select, beams, preferred_element_type=jnp.float32).astype(
        jnp.bfloat16
    )
    placed = placed.reshape(n_chan, most, 2, ch_dev, spectra_n)
    resynth = resynthesize(
        lax.all_to_all(placed, "chan", split_axis=0, concat_axis=3, tiled=True)[0],
        table,
        taps_count,
        chans,
    )
    return (visibility, resynth)


def solution(mesh):
    placed = (
        P(("grp", "chan", "sub"), None, None),
        P(),
        P(),
        P("grp"),
        P(("grp", "sub"), None),
        P("grp", None),
    )
    return jax.shard_map(
        local,
        mesh=mesh,
        in_specs=placed,
        out_specs=(P(("grp", "chan"), None, "sub", None), P(("grp", "chan", "sub"), None, None)),
        check_vma=False,
    )
```

profile of v0, /device:TPU:0, one launch (start us, length us, event | category | flops | bytes accessed | tf_op | source)
XLA Modules:
  0.0 464.1 jit_solution(4813590015660750824)
XLA Ops:
  8.0 3.7 reshape.232
  16.0 4.7 %negate_convert_fusion.1 = (bf16[1536,128]{1,0:T(8,128)(2,1)S(1)}, bf16[1536,128]{1,0:T(8,128)(2,1)S(1)}, bf16[1536,128]{1,0:T(8,128)(2,1)S(1)}) fusion(s32[1536]{0:T(1024)S(1)} %add_select_fusion.3, f32[1536]{0:T(1024)S(1)} %copy-done.4), kind=kLoop, calls=%fused_computation.79 | loop fusion | flops 3932160 | bytes 1191936 | tf_op jit(solution)/shard_map/convert.13
  30.2 4.8 %copy-done.3 = bf16[64,2,32,1536]{3,0,1,2:T(8,128)(2,1)} copy-done((bf16[64,2,32,1536]{3,0,1,2:T(8,128)(2,1)}, bf16[64,2,32,1536]{3,0,1,2:T(8,128)(2,1)S(1)}, u32[]{:S(2)}) %copy-start.3) | copy-done | bytes 12582936
  35.1 8.2 %fusion.15 = bf16[256,64,32]{0,1,2:T(8,128)(2,1)S(1)} fusion(bf16[2,1536,256,1]{2,1,0,3:T(8,128)(2,1)S(1)} %bitcast.153, bf16[64,2,32,1536]{3,0,1,2:T(8,128)(2,1)} %copy-done.3, f32[32]{0:T(128)S(1)} %compare_convert_fusion), kind=kOutput, calls=%fused_computation.28 | convolution fusion | flops 3222274048 | bytes 15204480 | tf_op jit(solution)/shard_map/icth,chm->mit/dot_general | solution.py:65
  47.5 32.0 %all_to_all.33 = bf16[4,2,65536]{2,1,0:T(2,128)(2,1)} all-to-all(bf16[4,2,65536]{2,1,0:T(2,128)(2,1)S(1)} %reshape.237), channel_id=1, replica_groups=mesh['grp'=2,'chan'=4,'sub'=4] {'chan'}, dimensions={0} | all-to-all | bytes 2097152 | tf_op jit(solution)/shard_map/all_to_all | solution.py:69
  82.6 6.5 %copy.149 = bf16[2,32,4,64,32]{4,1,3,2,0:T(8,128)(2,1)} copy(bf16[2,32,4,64,32]{3,4,0,1,2:T(8,128)(2,1)S(1)} %bitcast.149) | data formatting | bytes 2097152 | tf_op jit(solution)/shard_map/all_to_all | solution.py:69
  89.2 4.3 scatter_custom_fusion
  94.5 4.2 negate_convert_fusion
  99.9 94.3 %all-gather.2.cloned.1.call-done = bf16[2,32,1024,32]{3,1,2,0:T(8,128)(2,1)} async-done(((bf16[2,32,256,32]{3,1,2,0:T(8,128)(2,1)}), bf16[2,32,1024,32]{3,1,2,0:T(8,128)(2,1)}) %all-gather.2.cloned.1.call-update) | async-done | bytes 4194320 | tf_op jit(solution)/shard_map/all_gather | solution.py:70
  194.3 19.1 %gather_fusion = bf16[1024,2,32,32]{3,2,1,0:T(8,128)(2,1)} fusion(bf16[2,32,1024,32]{3,1,2,0:T(8,128)(2,1)} %all-gather.2.cloned.1.call-done, s32[1024]{0:T(1024)S(1)} %broadcast_clamp_fusion), kind=kCustom, calls=%fused_computation | custom fusion | bytes 8392704 | tf_op jit(solution)/shard_map/jit(_take)/gather | solution.py:74
  213.4 17.5 %copy.109 = bf16[1024,2,32,32]{0,3,1,2:T(8,128)(2,1)} copy(bf16[1024,2,32,32]{3,2,1,0:T(8,128)(2,1)} %gather_fusion) | data formatting | bytes 8388608 | tf_op jit(solution)/shard_map/jit(_take)/gather | solution.py:74
  237.0 31.8 %fusion.21 = f32[2,32,64,32]{2,3,0,1:T(8,128)S(1)} fusion(s32[32]{0:T(128)S(1)} %iota_add_fusion, s32[64,1024]{1,0:T(8,128)S(1)} %copy-done.8, bf16[1024,2,32,32]{0,3,1,2:T(8,128)(2,1)S(1)} %broadcast_select_fusion), kind=kOutput, calls=%fused_computation.35 | convolution fusion | flops 301989888 | bytes 4980864 | tf_op jit(solution)/shard_map/xbi,cxit->cxbt/dot_general | solution.py:90
  268.8 32.1 %fusion.18 = f32[2,32,64,32]{2,3,0,1:T(8,128)S(1)} fusion(s32[32]{0:T(128)S(1)} %iota_add_fusion, s32[64,1024]{1,0:T(8,128)S(1)} %copy-done.8, bf16[1024,2,32,32]{0,3,1,2:T(8,128)(2,1)S(1)} %broadcast_select_fusion), kind=kOutput, calls=%fused_computation.34 | convolution fusion | flops 301989888 | bytes 4980864 | tf_op jit(solution)/shard_map/xbi,cxit->cxbt/dot_general | solution.py:91
  307.3 4.5 reshape.239
  311.8 4.6 all-to-all-start.1
  316.4 15.5 %convolution_bitcast_fusion = f32[32,1,256,1024]{3,2,0,1:T(8,128)} fusion(bf16[2,32,256,32]{2,3,0,1:T(8,128)(2,1)S(1)} %dynamic-slice_bitcast_fusion, bf16[1024,2,32,32]{0,3,1,2:T(8,128)(2,1)} %copy-done.1), kind=kOutput, calls=%fused_computation.8 | convolution fusion | flops 1073741824 | bytes 38797312 | tf_op jit(solution)/shard_map/cxit,cxjt->xij/dot_general | solution.py:77
  331.8 14.0 %fusion.14 = f32[32,256,1024]{2,1,0:T(8,128)} fusion(bf16[2,32,1024,32]{2,3,0,1:T(8,128)(2,1)S(1)} %copy-done.2, bf16[2,32,256,32]{2,3,0,1:T(8,128)(2,1)S(1)} %dynamic-slice_bitcast_fusion), kind=kOutput, calls=%fused_computation.26 | convolution fusion | flops 536870912 | bytes 36175872 | tf_op jit(solution)/shard_map/xit,xjt->xij/dot_general | solution.py:78
  345.9 21.7 %subtract_bitcast_fusion = f32[32,1,256,1024]{3,2,0,1:T(8,128)} fusion(f32[32,256,1024]{2,1,0:T(8,128)} %fusion.14, bf16[2,32,1024,32]{2,3,0,1:T(8,128)(2,1)S(1)} %copy-done.2, bf16[2,32,256,32]{2,3,0,1:T(8,128)(2,1)S(1)} %dynamic-slice_bitcast_fusion), kind=kOutput, calls=%fused_computation.4 | convolution fusion | flops 545259520 | bytes 69730304 | tf_op jit(solution)/shard_map/xit,xjt->xij/dot_general | solution.py:79
  367.5 33.5 %fusion = bf16[32,2,256,1024]{3,2,0,1:T(8,128)(2,1)} fusion(f32[32,1,256,1024]{3,2,0,1:T(8,128)} %subtract_bitcast_fusion, f32[32,1,256,1024]{3,2,0,1:T(8,128)} %convolution_bitcast_fusion, f32[]{:T(128)} %convert_reduce_fusion.1), kind=kLoop, calls=%fused_computation.3 | loop fusion | flops 50331648 | bytes 100663296 | tf_op jit(solution)/shard_map/convert_element_type | solution.py:82
  401.1 23.2 %copy.126 = bf16[32,2,256,1024]{3,2,1,0:T(8,128)(2,1)} copy(bf16[32,2,256,1024]{3,2,0,1:T(8,128)(2,1)} %fusion) | data formatting | bytes 67108864
  427.2 5.2 %copy.112 = bf16[1,32,2,4,32,32]{4,3,5,2,1,0:T(4,128)(2,1)S(1)} copy(bf16[1,32,2,4,32,32]{1,5,4,2,3,0:T(8,128)(2,1)} %bitcast_bitcast_fusion) | data formatting | bytes 1048576 | tf_op jit(solution)/shard_map/all_to_all | solution.py:106
  433.5 7.4 %convolution_bitcast_fusion.1 = f32[32,32,2,12,128]{4,1,3,2,0:T(8,128)} fusion(bf16[2,12,128,2,128]{4,2,1,0,3:T(8,128)(2,1)} %bitcast.152, bf16[32,2,128,32,1,1]{2,3,1,0,4,5:T(8,128)(2,1)S(1)} %reshape.229), kind=kOutput, calls=%fused_computation.16 | convolution fusion | flops 1610612736 | bytes 14680064 | tf_op jit(solution)/shard_map/pcht,mch->ptm/dot_general | solution.py:32
  440.9 9.1 %slice_bitcast_fusion.15 = (f32[32,32,2,128]{3,1,2,0:T(8,128)S(1)}, f32[32,32,2,128]{3,1,2,0:T(8,128)S(1)}, f32[32,32,2,128]{3,1,2,0:T(8,128)S(1)}, f32[32,32,2,...) fusion(f32[32,32,2,12,128]{4,1,3,2,0:T(8,128)} %convolution_bit, ...), kind=kLoop, calls=%fused_computation.54 | loop fusion | bytes 25165824 | tf_op jit(solution)/shard_map/squeeze | solution.py:37
  450.0 5.0 %add_bitcast_fusion = f32[32,2,43,128]{3,2,1,0:T(8,128)S(1)} fusion(f32[32,32,2,128]{3,1,2,0:T(8,128)} %get-tuple-element.22, f32[32,32,2,128]{3,1,2,0:T(8,128)} %get-tuple-element.23, f32[32,32,2,128]{3,1,2,0:T(8,128)S(1)} %get-tuple-element.13, f32[32,32,2,128]{3,1,2,0:T(8,128)S(1)} %get-tuple-element.14, f32[32,32,2,128]{3,1,2,0:T(8,128)S(1)} %get-tuple-element.15, ...), kind=kLoop, calls=%fused_computation.33 | loop fusion | flops 3874816 | bytes 13991936 | tf_op jit(solution)/shard_map/transpose | solution.py:39
  (63 shorter events, 42.4 us)
Async XLA Ops:
  7.2 187.1 %all-gather.2.cloned.1.call-start = ((), (), s32[]{:S(2)}) async-start(), calls=%async_computation.2 | async-start | bytes 20971520 | tf_op jit(solution)/shard_map/all_gather | solution.py:70
  11.7 4.2 copy-start.4
  30.2 4.8 %copy-start.3 = (bf16[64,2,32,1536]{3,0,1,2:T(8,128)(2,1)}, bf16[64,2,32,1536]{3,0,1,2:T(8,128)(2,1)S(1)}, u32[]{:S(2)}) copy-start(bf16[64,2,32,1536]{3,0,1,2:T(8,128)(2,1)S(1)} %copy_dynamic-update-slice_fusion) | copy-start | bytes 37748740
  82.6 6.6 %copy-start.5 = (s32[1024]{0:T(1024)S(1)}, s32[1024]{0:T(1024)}, u32[]{:S(2)}) copy-start(s32[1024]{0:T(1024)} %param.8) | copy-start | bytes 12292
  82.6 10.9 %copy-start.7 = (s32[256,1]{0,1:T(1,128)S(1)}, s32[256,1]{0,1:T(1,128)}, u32[]{:S(2)}) copy-start(s32[256,1]{0,1:T(1,128)} %param.11) | copy-start | bytes 3076
  82.6 11.0 %copy-start.6 = (s32[4]{0:T(128)S(1)}, s32[4]{0:T(128)}, u32[]{:S(2)}) copy-start(s32[4]{0:T(128)} %param.9) | copy-start | bytes 52
  230.9 3.4 copy-start
  234.4 66.6 %copy-start.1 = (bf16[1024,2,32,32]{0,3,1,2:T(8,128)(2,1)}, bf16[1024,2,32,32]{0,3,1,2:T(8,128)(2,1)S(1)}, u32[]{:S(2)}) copy-start(bf16[1024,2,32,32]{0,3,1,2:T(8,128)(2,1)S(1)} %broadcast_select_fusion) | copy-start | bytes 12582916
  234.4 2.7 copy-start.8
  311.8 112.5 %all-to-all-start.1 = ((bf16[4,2,32768]{2,1,0:T(2,128)(2,1)}), bf16[4,2,32768]{2,1,0:T(2,128)(2,1)S(1)}, u32[]{:S(2)}, u32[]{:S(2)}) async-start(bf16[4,2,32768]{2,1,0:T(2,128)(2,1)} %reshape.239), calls=%async_computation.1 | async-start | bytes 1048576 | tf_op jit(solution)/shard_map/all_to_all | solution.py:106
  316.4 15.5 %copy-start.2 = (bf16[2,32,1024,32]{2,3,0,1:T(8,128)(2,1)S(1)}, bf16[2,32,1024,32]{2,3,0,1:T(8,128)(2,1)}, u32[]{:S(2)}) copy-start(bf16[2,32,1024,32]{2,3,0,1:T(8,128)(2,1)} %fusion.78) | copy-start | bytes 12582916
Sparse Core Ops, SparseCore 0:
  89.2 104.9 all-gather.1
where the time goes:
time: 469 us; the launch traced here: 464 us
  matrix products  132 us (28%)
  local copies, waits for them, and re-layouts  131 us (28%)
  waiting for transfers between devices  94.4 us (20%)
  other arithmetic  55.3 us (12%)
  blocking collectives  32 us (7%)
  between operations  14.9 us (3%)
    all_gather x1, waiting for transfers between devices, local(): gathered = lax.all_gather(turned, 'sub', axis=2, tiled=True)  94.3 us
    unnamed x34, local copies, waits for them, and re-layouts  48.3 us
    gather x2, local copies, waits for them, and re-layouts, local(): by_id = jnp.take(gathered, order, axis=2)  36.6 us
    convert_element_type x1, other arithmetic, local(): (jnp.stack([real_part, imag_part], axis=1) / total).astype(jnp.bfloat16)  33.5 us
    dot_general x1, matrix products, local(): jnp.einsum('xbi,cxit->cxbt', weight_sin, by_id, preferred_element_type=jn...  32.1 us
    all_to_all x1, blocking collectives, local(): lax.all_to_all(spectra, 'chan', split_axis=1, concat_axis=2, tiled=True)  32 us
    dot_general x1, matrix products, local(): jnp.einsum('xbi,cxit->cxbt', weight_cos, by_id, preferred_element_type=jn...  31.8 us
    dot_general x1, matrix products, local(): jnp.einsum('xit,xjt->xij', mine[0], by_id[1], preferred_element_type=jnp....  21.7 us
  transfers between devices with their start and end apart: 2, of which 1 were waited for; matrix products, arithmetic and copies ran while one was open for 26% of the time, Pallas kernels for 0%

commit v1 on v0

--- a/solution.py
+++ b/solution.py
@@ -67,7 +67,12 @@
     spectra = filtered.reshape(2, chans, inp_dev, spectra_n).astype(jnp.bfloat16)
     slot_of = jnp.zeros((inputs,), jnp.int32).at[input_id].set(jnp.arange(inputs, dtype=jnp.int32))
     turned = lax.all_to_all(spectra, "chan", split_axis=1, concat_axis=2, tiled=True)
-    gathered = lax.all_gather(turned, "sub", axis=2, tiled=True)
+    ring = [turned]
+    for hop in range(3):
+        ring.append(lax.ppermute(ring[-1], "sub", [(dev, (dev + 1) % 4) for dev in range(4)]))
+    gathered = jnp.roll(
+        jnp.concatenate(ring[::-1], axis=2), (lax.axis_index("sub") + 1) * ring[0].shape[2], axis=2
+    )
     chan_part = slot_of // (n_sub * inp_dev)
     sub_part = slot_of // inp_dev % n_sub
     order = (sub_part * n_chan + chan_part) * inp_dev + slot_of % inp_dev

time: 469 us -> 420 us (0.90)
  waiting for transfers between devices: 94.4 us -> 31.9 us
  local copies, waits for them, and re-layouts: 131 us -> 159 us
  between operations: 14.9 us -> 1.56 us
    all_gather x1 -> x0, waiting for transfers between devices: 94.3 us -> none  [local(): gathered = lax.all_gather(turned, 'sub', axis=2, tiled=True)]
    ppermute x0 -> x3, waiting for transfers between devices: none -> 31.9 us  [local(): lax.ppermute(ring[-1], 'sub', [(dev, (dev + 1) % 4) for dev in range(4)])]
    unnamed x34 -> x42, local copies, waits for them, and re-layouts: 48.3 us -> 72.4 us
  transfers between devices with their start and end apart: 2 -> 4, of which waited for: 1 -> 3; matrix products, arithmetic and copies ran while one was open for 26% -> 29% of each run, Pallas kernels for 0% -> 0%
where the time goes in v1:
time: 420 us; the launch traced here: 415 us
  local copies, waits for them, and re-layouts  159 us (38%)
  matrix products  132 us (31%)
  other arithmetic  55.3 us (13%)
  blocking collectives  32 us (8%)
  waiting for transfers between devices  31.9 us (8%)
    unnamed x42, local copies, waits for them, and re-layouts  72.4 us
    gather x2, local copies, waits for them, and re-layouts, local(): by_id = jnp.take(gathered, order, axis=2)  36.6 us
    convert_element_type x1, other arithmetic, local(): (jnp.stack([real_part, imag_part], axis=1) / total).astype(jnp.bfloat16)  33.5 us
    dot_general x1, matrix products, local(): jnp.einsum('xbi,cxit->cxbt', weight_sin, by_id, preferred_element_type=jn...  32.1 us
    all_to_all x1, blocking collectives, local(): lax.all_to_all(spectra, 'chan', split_axis=1, concat_axis=2, tiled=True)  32 us
    ppermute x3, waiting for transfers between devices, local(): lax.ppermute(ring[-1], 'sub', [(dev, (dev + 1) % 4) for dev in range(4)])  31.9 us
    dot_general x1, matrix products, local(): jnp.einsum('xbi,cxit->cxbt', weight_cos, by_id, preferred_element_type=jn...  31.8 us
    dot_general x1, matrix products, local(): jnp.einsum('xit,xjt->xij', mine[0], by_id[1], preferred_element_type=jnp....  21.7 us
  transfers between devices with their start and end apart: 4, of which 3 were waited for; matrix products, arithmetic and copies ran while one was open for 29% of the time, Pallas kernels for 0%

profile of v1, /device:TPU:0, one launch (start us, length us, event | category | flops | bytes accessed | tf_op | source)
XLA Modules:
  0.0 414.9 jit_solution(3495637298301646917)
XLA Ops:
  9.4 4.7 %negate_convert_fusion.1 = (bf16[1536,128]{1,0:T(8,128)(2,1)S(1)}, bf16[1536,128]{1,0:T(8,128)(2,1)S(1)}, bf16[1536,128]{1,0:T(8,128)(2,1)S(1)}) fusion(s32[1536]{0:T(1024)S(1)} %add_select_fusion.3, f32[1536]{0:T(1024)S(1)} %copy-done.4), kind=kLoop, calls=%fused_computation.79 | loop fusion | flops 3932160 | bytes 1191936 | tf_op jit(solution)/shard_map/convert.13
  23.6 4.8 %copy-done.3 = bf16[64,2,32,1536]{3,0,1,2:T(8,128)(2,1)} copy-done((bf16[64,2,32,1536]{3,0,1,2:T(8,128)(2,1)}, bf16[64,2,32,1536]{3,0,1,2:T(8,128)(2,1)S(1)}, u32[]{:S(2)}) %copy-start.3) | copy-done | bytes 12582936
  28.5 8.3 %fusion.15 = bf16[256,64,32]{0,1,2:T(8,128)(2,1)S(1)} fusion(bf16[2,1536,256,1]{2,1,0,3:T(8,128)(2,1)S(1)} %bitcast.153, bf16[64,2,32,1536]{3,0,1,2:T(8,128)(2,1)} %copy-done.3, f32[32]{0:T(128)S(1)} %compare_convert_fusion), kind=kOutput, calls=%fused_computation.28 | convolution fusion | flops 3222274048 | bytes 15204480 | tf_op jit(solution)/shard_map/icth,chm->mit/dot_general | solution.py:65
  41.0 32.0 %all_to_all.33 = bf16[4,2,65536]{2,1,0:T(2,128)(2,1)} all-to-all(bf16[4,2,65536]{2,1,0:T(2,128)(2,1)S(1)} %reshape.237), channel_id=1, replica_groups=mesh['grp'=2,'chan'=4,'sub'=4] {'chan'}, dimensions={0} | all-to-all | bytes 2097152 | tf_op jit(solution)/shard_map/all_to_all | solution.py:69
  83.6 14.2 %collective-permute-done = bf16[2,32,256,32]{2,3,1,0:T(8,128)(2,1)S(1)} collective-permute-done((bf16[2,32,256,32]{2,3,1,0:T(8,128)(2,1)S(1)}, bf16[2,32,256,32]{2,3,1,0:T(8,128)(2,1)S(1)}, u32[]{:S(2)}, u32[]{:S(2)}) %collective-permute-start) | collective-permute-done | bytes 1048608 | tf_op jit(solution)/shard_map/ppermute | solution.py:72
  97.8 4.3 %scatter_custom_fusion = s32[1024]{0:T(1024)S(1)} fusion(s32[1024]{0:T(1024)S(1)} %compare_select_fusion.1, s32[1024]{0:T(1024)S(1)} %iota.42, s32[]{:T(128)} %constant.132.clone.1), kind=kCustom, calls=%fused_computation.142 | custom fusion | bytes 4100 | tf_op jit(solution)/shard_map/scatter | solution.py:68
  103.1 8.9 %collective-permute-done.1 = bf16[2,32,256,32]{2,3,1,0:T(8,128)(2,1)S(1)} collective-permute-done((bf16[2,32,256,32]{2,3,1,0:T(8,128)(2,1)S(1)}, bf16[2,32,256,32]{2,3,1,0:T(8,128)(2,1)S(1)}, u32[]{:S(2)}, u32[]{:S(2)}) %collective-permute-start.1) | collective-permute-done | bytes 1048608 | tf_op jit(solution)/shard_map/ppermute | solution.py:72
  112.1 4.1 negate_convert_fusion
  117.5 8.7 %collective-permute-done.2 = bf16[2,32,256,32]{2,3,1,0:T(8,128)(2,1)S(1)} collective-permute-done((bf16[2,32,256,32]{2,3,1,0:T(8,128)(2,1)S(1)}, bf16[2,32,256,32]{2,3,1,0:T(8,128)(2,1)S(1)}, u32[]{:S(2)}, u32[]{:S(2)}) %collective-permute-start.2) | collective-permute-done | bytes 1048608 | tf_op jit(solution)/shard_map/ppermute | solution.py:72
  130.0 23.0 %copy.164 = bf16[2,32,1024,32]{3,1,2,0:T(8,128)(2,1)} copy(bf16[2,32,1024,32]{2,3,1,0:T(8,128)(2,1)} %constant_dynamic-slice_fusion.1) | data formatting | bytes 8388608
  153.0 19.2 %gather_fusion = bf16[1024,2,32,32]{3,2,1,0:T(8,128)(2,1)} fusion(bf16[2,32,1024,32]{3,1,2,0:T(8,128)(2,1)} %copy.164, s32[1024]{0:T(1024)S(1)} %broadcast_clamp_fusion), kind=kCustom, calls=%fused_computation | custom fusion | bytes 8392704 | tf_op jit(solution)/shard_map/jit(_take)/gather | solution.py:79
  172.2 17.5 %copy.111 = bf16[1024,2,32,32]{0,3,1,2:T(8,128)(2,1)} copy(bf16[1024,2,32,32]{3,2,1,0:T(8,128)(2,1)} %gather_fusion) | data formatting | bytes 8388608 | tf_op jit(solution)/shard_map/jit(_take)/gather | solution.py:79
  195.7 31.8 %fusion.21 = f32[2,32,64,32]{2,3,0,1:T(8,128)S(1)} fusion(s32[32]{0:T(128)S(1)} %iota_add_fusion, s32[64,1024]{1,0:T(8,128)S(1)} %copy-done.8, bf16[1024,2,32,32]{0,3,1,2:T(8,128)(2,1)S(1)} %broadcast_select_fusion), kind=kOutput, calls=%fused_computation.35 | convolution fusion | flops 301989888 | bytes 4980864 | tf_op jit(solution)/shard_map/xbi,cxit->cxbt/dot_general | solution.py:95
  227.5 32.1 %fusion.18 = f32[2,32,64,32]{2,3,0,1:T(8,128)S(1)} fusion(s32[32]{0:T(128)S(1)} %iota_add_fusion, s32[64,1024]{1,0:T(8,128)S(1)} %copy-done.8, bf16[1024,2,32,32]{0,3,1,2:T(8,128)(2,1)S(1)} %broadcast_select_fusion), kind=kOutput, calls=%fused_computation.34 | convolution fusion | flops 301989888 | bytes 4980864 | tf_op jit(solution)/shard_map/xbi,cxit->cxbt/dot_general | solution.py:96
  266.0 4.5 %reshape.239 = bf16[4,2,32768]{2,1,0:T(2,128)(2,1)} reshape(bf16[4,2,32,32,32]{4,3,2,1,0:T(8,128)(2,1)} %bitcast.150) | data formatting | bytes 1048576
  274.0 15.5 %convolution_bitcast_fusion = f32[32,1,256,1024]{3,2,0,1:T(8,128)} fusion(bf16[2,32,256,32]{2,3,0,1:T(8,128)(2,1)S(1)} %dynamic-slice_bitcast_fusion, bf16[1024,2,32,32]{0,3,1,2:T(8,128)(2,1)} %copy-done.1), kind=kOutput, calls=%fused_computation.8 | convolution fusion | flops 1073741824 | bytes 38797312 | tf_op jit(solution)/shard_map/cxit,cxjt->xij/dot_general | solution.py:82
  289.4 14.0 %fusion.14 = f32[32,256,1024]{2,1,0:T(8,128)} fusion(bf16[2,32,1024,32]{2,3,0,1:T(8,128)(2,1)S(1)} %copy-done.2, bf16[2,32,256,32]{2,3,0,1:T(8,128)(2,1)S(1)} %dynamic-slice_bitcast_fusion), kind=kOutput, calls=%fused_computation.26 | convolution fusion | flops 536870912 | bytes 36175872 | tf_op jit(solution)/shard_map/xit,xjt->xij/dot_general | solution.py:83
  303.5 21.7 %subtract_bitcast_fusion = f32[32,1,256,1024]{3,2,0,1:T(8,128)} fusion(f32[32,256,1024]{2,1,0:T(8,128)} %fusion.14, bf16[2,32,1024,32]{2,3,0,1:T(8,128)(2,1)S(1)} %copy-done.2, bf16[2,32,256,32]{2,3,0,1:T(8,128)(2,1)S(1)} %dynamic-slice_bitcast_fusion), kind=kOutput, calls=%fused_computation.4 | convolution fusion | flops 545259520 | bytes 69730304 | tf_op jit(solution)/shard_map/xit,xjt->xij/dot_general | solution.py:84
  325.1 33.5 %fusion = bf16[32,2,256,1024]{3,2,0,1:T(8,128)(2,1)} fusion(f32[32,1,256,1024]{3,2,0,1:T(8,128)} %subtract_bitcast_fusion, f32[32,1,256,1024]{3,2,0,1:T(8,128)} %convolution_bitcast_fusion, f32[]{:T(128)} %convert_reduce_fusion.1), kind=kLoop, calls=%fused_computation.3 | loop fusion | flops 50331648 | bytes 100663296 | tf_op jit(solution)/shard_map/convert_element_type | solution.py:87
  358.7 23.2 %copy.128 = bf16[32,2,256,1024]{3,2,1,0:T(8,128)(2,1)} copy(bf16[32,2,256,1024]{3,2,0,1:T(8,128)(2,1)} %fusion) | data formatting | bytes 67108864
  384.8 5.2 %copy.114 = bf16[1,32,2,4,32,32]{4,3,5,2,1,0:T(4,128)(2,1)S(1)} copy(bf16[1,32,2,4,32,32]{1,5,4,2,3,0:T(8,128)(2,1)} %bitcast_bitcast_fusion) | data formatting | bytes 1048576 | tf_op jit(solution)/shard_map/all_to_all | solution.py:111
  391.1 7.4 %convolution_bitcast_fusion.1 = f32[32,32,2,12,128]{4,1,3,2,0:T(8,128)} fusion(bf16[2,12,128,2,128]{4,2,1,0,3:T(8,128)(2,1)} %bitcast.152, bf16[32,2,128,32,1,1]{2,3,1,0,4,5:T(8,128)(2,1)S(1)} %reshape.229), kind=kOutput, calls=%fused_computation.16 | convolution fusion | flops 1610612736 | bytes 14680064 | tf_op jit(solution)/shard_map/pcht,mch->ptm/dot_general | solution.py:32
  398.5 9.1 %slice_bitcast_fusion.15 = (f32[32,32,2,128]{3,1,2,0:T(8,128)S(1)}, f32[32,32,2,128]{3,1,2,0:T(8,128)S(1)}, f32[32,32,2,128]{3,1,2,0:T(8,128)S(1)}, f32[32,32,2,...) fusion(f32[32,32,2,12,128]{4,1,3,2,0:T(8,128)} %convolution_bit, ...), kind=kLoop, calls=%fused_computation.54 | loop fusion | bytes 25165824 | tf_op jit(solution)/shard_map/squeeze | solution.py:37
  407.6 5.0 %add_bitcast_fusion = f32[32,2,43,128]{3,2,1,0:T(8,128)S(1)} fusion(f32[32,32,2,128]{3,1,2,0:T(8,128)} %get-tuple-element.22, f32[32,32,2,128]{3,1,2,0:T(8,128)} %get-tuple-element.23, f32[32,32,2,128]{3,1,2,0:T(8,128)S(1)} %get-tuple-element.13, f32[32,32,2,128]{3,1,2,0:T(8,128)S(1)} %get-tuple-element.14, f32[32,32,2,128]{3,1,2,0:T(8,128)S(1)} %get-tuple-element.15, ...), kind=kLoop, calls=%fused_computation.33 | loop fusion | flops 3874816 | bytes 13991936 | tf_op jit(solution)/shard_map/transpose | solution.py:39
  (77 shorter events, 60.7 us)
Async XLA Ops:
  5.1 4.2 %copy-start.4 = (f32[1536]{0:T(1024)S(1)}, f32[1536]{0:T(1024)}, u32[]{:S(2)}) copy-start(f32[1536]{0:T(1024)} %param.7) | copy-start | bytes 18436
  23.6 4.8 %copy-start.3 = (bf16[64,2,32,1536]{3,0,1,2:T(8,128)(2,1)}, bf16[64,2,32,1536]{3,0,1,2:T(8,128)(2,1)S(1)}, u32[]{:S(2)}) copy-start(bf16[64,2,32,1536]{3,0,1,2:T(8,128)(2,1)S(1)} %copy_dynamic-update-slice_fusion) | copy-start | bytes 37748740
  39.3 58.6 %copy-start.5 = (s32[1024]{0:T(1024)S(1)}, s32[1024]{0:T(1024)}, u32[]{:S(2)}) copy-start(s32[1024]{0:T(1024)} %param.8) | copy-start | bytes 12292
  39.3 62.9 %copy-start.7 = (s32[256,1]{0,1:T(1,128)S(1)}, s32[256,1]{0,1:T(1,128)}, u32[]{:S(2)}) copy-start(s32[256,1]{0,1:T(1,128)} %param.11) | copy-start | bytes 3076
  39.3 63.0 %copy-start.6 = (s32[4]{0:T(128)S(1)}, s32[4]{0:T(128)}, u32[]{:S(2)}) copy-start(s32[4]{0:T(128)} %param.9) | copy-start | bytes 52
  83.5 14.3 %collective-permute-start = (bf16[2,32,256,32]{2,3,1,0:T(8,128)(2,1)S(1)}, bf16[2,32,256,32]{2,3,1,0:T(8,128)(2,1)S(1)}, u32[]{:S(2)}, u32[]{:S(2)}) collective-permute-start(bf16[2,32,256,32]{2,3,1,0:T(8,128)(2,1)S(1)} %all_to_all.27), channel_id=1, source_target_pairs={{0,1},{1,2},{2,3},{3,0},{4,5},{5,6},{6,7},{7,4},{8,9},{9,10},{10,1... | collective-permute-start | bytes 3145736 | tf_op jit(solution)/shard_map/ppermute | solution.py:72
  97.8 14.2 %collective-permute-start.1 = (bf16[2,32,256,32]{2,3,1,0:T(8,128)(2,1)S(1)}, bf16[2,32,256,32]{2,3,1,0:T(8,128)(2,1)S(1)}, u32[]{:S(2)}, u32[]{:S(2)}) collective-permute-start(bf16[2,32,256,32]{2,3,1,0:T(8,128)(2,1)S(1)} %collective-permute-done), channel_id=1, source_target_pairs={{0,1},{1,2},{2,3},{3,0},{4,5},{5,6},{6,7},{7,4},{8,9},{9,10},{10,1... | collective-permute-start | bytes 3145736 | tf_op jit(solution)/shard_map/ppermute | solution.py:72
  112.0 14.2 %collective-permute-start.2 = (bf16[2,32,256,32]{2,3,1,0:T(8,128)(2,1)S(1)}, bf16[2,32,256,32]{2,3,1,0:T(8,128)(2,1)S(1)}, u32[]{:S(2)}, u32[]{:S(2)}) collective-permute-start(bf16[2,32,256,32]{2,3,1,0:T(8,128)(2,1)S(1)} %collective-permute-done.1), channel_id=1, source_target_pairs={{0,1},{1,2},{2,3},{3,0},{4,5},{5,6},{6,7},{7,4},{8,9},{9,10},{10,1... | collective-permute-start | bytes 3145736 | tf_op jit(solution)/shard_map/ppermute | solution.py:72
  189.6 3.4 copy-start
  189.6 6.1 %copy-start.8 = (s32[64,1024]{1,0:T(8,128)S(1)}, s32[64,1024]{1,0:T(8,128)}, u32[]{:S(2)}) copy-start(s32[64,1024]{1,0:T(8,128)} %param.10) | copy-start | bytes 786436
  193.1 66.5 %copy-start.1 = (bf16[1024,2,32,32]{0,3,1,2:T(8,128)(2,1)}, bf16[1024,2,32,32]{0,3,1,2:T(8,128)(2,1)S(1)}, u32[]{:S(2)}) copy-start(bf16[1024,2,32,32]{0,3,1,2:T(8,128)(2,1)S(1)} %broadcast_select_fusion) | copy-start | bytes 12582916
  270.5 111.5 %all-to-all-start.1 = ((bf16[4,2,32768]{2,1,0:T(2,128)(2,1)}), bf16[4,2,32768]{2,1,0:T(2,128)(2,1)S(1)}, u32[]{:S(2)}, u32[]{:S(2)}) async-start(bf16[4,2,32768]{2,1,0:T(2,128)(2,1)} %reshape.239), calls=%async_computation.1 | async-start | bytes 1048576 | tf_op jit(solution)/shard_map/all_to_all | solution.py:111
  273.9 15.5 %copy-start.2 = (bf16[2,32,1024,32]{2,3,0,1:T(8,128)(2,1)S(1)}, bf16[2,32,1024,32]{2,3,0,1:T(8,128)(2,1)}, u32[]{:S(2)}) copy-start(bf16[2,32,1024,32]{2,3,0,1:T(8,128)(2,1)} %fusion.79) | copy-start | bytes 12582916
